TPU v7x, 32 devices: a whole 2x2x4 slice. The times are simulated.
32 devices in a mesh: groups: 2 (over y), sec: 4 (over z), tile: 2 (over x), row: 2 (over core).
Axes of the slice: x: 2, y: 2, z: 4, core: 2. Of those that a mesh axis runs over, the one named last changes fastest.
Arguments:
- section_pixels: float32 [8, 512, 4096], P(('groups', 'sec'), ('tile', 'row')), parts along dimension 0, may hold values from -40 to 40
- jitter_index: int32 [8, 512], P(('groups', 'sec'), ('tile', 'row')), parts along dimension 0, may hold values from 0 to 7
- drift_list: int32 [8, 4, 8, 3], P(('groups', 'sec')), parts along dimension 0, may hold values from 0 to 31, as said below
- blend_weight: float32 [8, 4, 8], P(('groups', 'sec')), parts along dimension 0, may hold values from 0.5 to 2
- patch_col: int32 [4, 8], P(('tile', 'row'), 'groups'), parts along dimension 1, may hold values from 0 to 896
Outputs:
- jitter_phase: float32 [8, 512], P(('groups', 'sec'), ('tile', 'row')), parts along dimension 0
- surfaces: float32 [6, 4, 4, 128, 128], P('groups', ('tile', 'row'), 'sec'), parts along dimension 0
There are 2 independent parts, one for each index of `groups`. A program takes and returns all parts, laid end to end along the dimension named above; each array names one. Nothing has to cross between parts.
Inputs may be any that keep to these rules, and one draw needn't show every extreme that they name: `drift_list`: entry [s, j, k] names a block of band j (distinct over k), the band that owns its target, and the target block. No band sends more than 2 blocks to one owner, and in every section one owner receives exactly 2 blocks from every band.
All inputs are finite; a program needn't handle non-finite values.
Results may differ from a plain program's by a relative error of at most 0.0065.
Values may be sent and summed in bfloat16 or wider, within the bound.
A program may use at most 64 MiB of HBM per device.

v0:
```python
import math

import jax
import jax.numpy as jnp
from jax import lax
from jax.sharding import PartitionSpec as P

SEG = 512
PATCH = 128
BLOCK = 128
JMAX = 8
OV = 8
CAP = 2


def shifted(block, axis, distance):
    devices = range(lax.axis_size(axis))
    route = [(i - distance, i) for i in devices if i - distance in devices]
    return lax.ppermute(block, axis, route)


def dft_tables(length):
    indices = jnp.arange(length, dtype=jnp.int32)
    products = indices[:, None] * indices[None, :] % length
    angles = products.astype(jnp.float32) * (2.0 * math.pi / length)
    return (jnp.cos(angles), jnp.sin(angles))


def align_rows(pixels, delays):
    row_width = pixels.shape[1]
    padded = jnp.pad(pixels, ((0, 0), (0, JMAX)))
    aligned = jnp.zeros_like(pixels)
    for shift_by in range(JMAX):
        aligned = aligned + jnp.where(
            delays[:, None] == shift_by, padded[:, shift_by : shift_by + row_width], 0.0
        )
    return aligned


def row_spectra(rows):
    row_count, row_width = rows.shape
    cosine_table, sine_table = dft_tables(SEG)
    dft_table = jnp.concatenate([cosine_table, -sine_table], 1)
    spectra = jnp.dot(
        rows.reshape(row_count * (row_width // SEG), SEG),
        dft_table,
        precision=lax.Precision.HIGHEST,
        preferred_element_type=jnp.float32,
    )
    spectra = spectra.reshape(row_count, row_width // SEG, 2 * SEG)
    return (spectra[..., :SEG], spectra[..., SEG:])


def jitter_estimate(now_real, now_imag, before_real, before_imag):
    indices = jnp.arange(SEG, dtype=jnp.int32)
    weights = jnp.sin(indices.astype(jnp.float32) * (2.0 * math.pi / SEG))
    cross_term = now_imag * before_real - now_real * before_imag
    numerator = jnp.mean(weights * cross_term, axis=(1, 2))
    power_sum = 0.5 * (
        now_real * now_real
        + now_imag * now_imag
        + before_real * before_real
        + before_imag * before_imag
    )
    return numerator / (jnp.mean(power_sum, axis=(1, 2)) + 1e-05)


def correct_rows(aligned, jitter):
    padded = jnp.pad(aligned, ((0, 0), (1, 1)))
    slopes = 0.5 * (padded[:, 2:] - padded[:, :-2])
    return (aligned - jitter[:, None] * slopes).astype(jnp.bfloat16)


def left_mul(matrix, batch):
    return jnp.einsum("ij,...jk->...ik", matrix, batch, precision=lax.Precision.HIGHEST)


def right_mul(batch, matrix):
    return jnp.einsum("...ij,jk->...ik", batch, matrix, precision=lax.Precision.HIGHEST)


def correlate(patches):
    side = patches.shape[-1]
    cosine_table, sine_table = dft_tables(side)
    values = patches.astype(jnp.float32)
    first_cos = right_mul(values, cosine_table)
    first_sin = right_mul(values, sine_table)
    freq_real = left_mul(cosine_table, first_cos) - left_mul(sine_table, first_sin)
    freq_imag = -(left_mul(sine_table, first_cos) + left_mul(cosine_table, first_sin))
    cross_real = freq_real[:-1] * freq_real[1:] + freq_imag[:-1] * freq_imag[1:]
    cross_imag = freq_imag[:-1] * freq_real[1:] - freq_real[:-1] * freq_imag[1:]
    magnitude = jnp.sqrt(cross_real * cross_real + cross_imag * cross_imag)
    damping = 0.5 * jnp.mean(magnitude, axis=(-2, -1), keepdims=True) + 1e-06
    scaled = 1.0 / (magnitude + damping)
    damped_real = cross_real * scaled
    damped_imag = cross_imag * scaled
    back_real = right_mul(damped_real, cosine_table) - right_mul(damped_imag, sine_table)
    back_imag = right_mul(damped_real, sine_table) + right_mul(damped_imag, cosine_table)
    return (left_mul(cosine_table, back_real) - left_mul(sine_table, back_imag)) / side


def per_device(section_pixels, jitter_index, drift_list, blend_weight, patch_col):
    pixels = section_pixels[0]
    row_count, row_width = pixels.shape
    aligned = align_rows(pixels, jitter_index[0])
    above_row = shifted(aligned[row_count - 1 :], ("tile", "row"), 1)
    now_real, now_imag = row_spectra(aligned)
    top_real, top_imag = row_spectra(above_row)
    before_real = jnp.concatenate([top_real, now_real[:-1]], 0)
    before_imag = jnp.concatenate([top_imag, now_imag[:-1]], 0)
    jitter = jitter_estimate(now_real, now_imag, before_real, before_imag)
    corrected = correct_rows(aligned, jitter)
    owners = lax.axis_size("tile") * lax.axis_size("row")
    owner_id = lax.axis_index("tile") * lax.axis_size("row") + lax.axis_index("row")
    blocks_across = row_width // BLOCK
    band_rows = row_count // BLOCK
    total_blocks = band_rows * blocks_across
    drifts = drift_list[0]
    weights = blend_weight[0]
    positions = jnp.arange(OV, dtype=jnp.int32)
    earlier = positions[None, :] < positions[:, None]
    same_owner = drifts[:, :, 1][:, :, None] == drifts[:, :, 1][:, None, :]
    slot_ids = jnp.sum((same_owner & earlier[None]).astype(jnp.int32), axis=2)
    my_list = lax.dynamic_index_in_dim(drifts, owner_id, 0, keepdims=False)
    my_slots = lax.dynamic_index_in_dim(slot_ids, owner_id, 0, keepdims=False)

    def cut_block(block_id):
        return lax.dynamic_slice(
            corrected,
            (block_id // blocks_across * BLOCK, block_id % blocks_across * BLOCK),
            (BLOCK, BLOCK),
        )

    sources = jax.vmap(cut_block)(my_list[:, 0])
    outgoing = (
        jnp.zeros((owners * CAP, BLOCK, BLOCK), jnp.bfloat16)
        .at[my_list[:, 1] * CAP + my_slots]
        .set(sources)
    )
    arrived = lax.all_to_all(
        outgoing.reshape(owners, CAP, BLOCK, BLOCK),
        ("tile", "row"),
        split_axis=0,
        concat_axis=0,
        tiled=True,
    )
    arrived = arrived.reshape(owners * CAP, BLOCK, BLOCK)
    to_me = (drifts[:, :, 1] == owner_id).astype(jnp.float32) * weights
    slot_index = (jnp.arange(owners, dtype=jnp.int32)[:, None] * CAP + slot_ids).reshape(-1)
    slot_onehot = (
        slot_index[:, None] == jnp.arange(owners * CAP, dtype=jnp.int32)[None, :]
    ).astype(jnp.float32)
    block_onehot = (
        jnp.arange(total_blocks, dtype=jnp.int32)[:, None] == drifts[:, :, 2].reshape(-1)[None, :]
    ).astype(jnp.float32)
    block_onehot = block_onehot * to_me.reshape(-1)[None, :]
    mixing = jnp.dot(
        block_onehot,
        slot_onehot,
        precision=lax.Precision.HIGHEST,
        preferred_element_type=jnp.float32,
    )
    incoming = jnp.einsum(
        "nm,mxy->nxy", mixing, arrived.astype(jnp.float32), precision=lax.Precision.HIGHEST
    )
    incoming = (
        incoming.reshape(band_rows, blocks_across, BLOCK, BLOCK)
        .transpose(0, 2, 1, 3)
        .reshape(row_count, row_width)
    )
    denominator = (1.0 + jnp.sum(block_onehot, axis=1)).reshape(band_rows, blocks_across)
    denominator = jnp.repeat(jnp.repeat(denominator, BLOCK, 0), BLOCK, 1)
    montage = ((corrected.astype(jnp.float32) + incoming) / denominator).astype(jnp.bfloat16)
    patch_rows = row_count // PATCH
    offsets = patch_col[0]
    slab_count = lax.axis_size("sec")
    slab_width = row_width // slab_count
    band_grid = montage.reshape(patch_rows, PATCH, slab_count, slab_width)
    picked = jax.vmap(
        lambda column_piece, start_col: lax.dynamic_slice_in_dim(column_piece, start_col, PATCH, 2),
        in_axes=(2, 0),
        out_axes=2,
    )(band_grid, offsets)
    outbound = picked.reshape(1, patch_rows, PATCH, slab_count * PATCH)
    surfaces = correlate(lax.all_to_all(outbound, "sec", split_axis=3, concat_axis=0, tiled=True))
    return (jitter[None, :], surfaces[:, :, None])


def solution(mesh):
    in_specs = (
        P(("groups", "sec"), ("tile", "row"), None),
        P(("groups", "sec"), ("tile", "row")),
        P(("groups", "sec"), None, None, None),
        P(("groups", "sec"), None, None),
        P(("tile", "row"), "groups"),
    )
    out_specs = (
        P(("groups", "sec"), ("tile", "row")),
        P("groups", ("tile", "row"), "sec", None, None),
    )
    return jax.shard_map(
        per_device, mesh=mesh, in_specs=in_specs, out_specs=out_specs, check_vma=False
    )
```

profile of v0, /device:TPU:0, one launch (start us, length us, event | category | flops | bytes accessed | tf_op | source)
XLA Modules:
  0.0 103.9 jit_solution(3331705832865443064)
XLA Ops:
  0.6 0.7 compare_bitcast_fusion.7
  1.3 2.9 %copy.89 = f32[1,128,4096]{1,2,0:T(8,128)} copy(f32[1,128,4096]{2,1,0:T(8,128)} %param.5) | data formatting | bytes 4194304 | tf_op args[0]
  4.2 9.1 %select_add_fusion = f32[128,4096]{0,1:T(8,128)S(1)} fusion(f32[128,4096]{0,1:T(8,128)} %bitcast.149, pred[128]{0:T(512)(128)(4,1)S(1)} %get-tuple-element.72, pred[128]{0:T(512)(128)(4,1)S(1)} %get-tuple-element.73, pred[128]{0:T(512)(128)(4,1)S(1)} %get-tuple-element.67, pred[128]{0:T(512)(128)(4,1)S(1)} %get-tuple-element.68, ...), kind=kLoop, calls=%fused_computation.17 | loop fusion | flops 7864320 | bytes 4195328 | tf_op jit(solution)/shard_map/add | solution.py:34
  13.3 2.0 %slice.124 = f32[1,4096]{0,1:T(8,128)} slice(f32[128,4096]{0,1:T(8,128)S(1)} %select_add_fusion), slice={[127:128], [0:4096]} | slice | bytes 32768 | tf_op jit(solution)/shard_map/slice | solution.py:106
  15.3 2.2 %copy.91 = f32[1,4096]{1,0:T(1,128)S(1)} copy(f32[1,4096]{0,1:T(8,128)} %slice.124) | data formatting | bytes 32768 | tf_op jit(solution)/shard_map/slice | solution.py:106
  17.5 2.4 %collective-permute-start = (f32[1,4096]{1,0:T(1,128)S(1)}, f32[1,4096]{1,0:T(1,128)S(1)}, u32[]{:S(2)}, u32[]{:S(2)}) collective-permute-start(f32[1,4096]{1,0:T(1,128)S(1)} %copy.91), channel_id=1, source_target_pairs={{0,1},{1,2},{2,3},{4,5},{5,6},{6,7},{8,9},{9,10},{10,11},{12,13},{... | collective-permute-start | bytes 49160 | tf_op jit(solution)/shard_map/ppermute | solution.py:19
  20.0 5.3 %sine_negate_fusion = (f32[512,512]{1,0:T(8,128)S(1)}, f32[512,512]{1,0:T(8,128)}) fusion(), kind=kLoop, calls=%fused_computation.37 | loop fusion | flops 3932160 | bytes 2097152 | tf_op jit(solution)/shard_map/neg | solution.py:43
  26.4 8.0 %fusion.2 = f32[128,8,1024]{2,0,1:T(8,128)S(1)} fusion(f32[128,8,512]{0,2,1:T(8,128)S(1)} %bitcast.148, f32[512,512]{1,0:T(8,128)S(1)} %get-tuple-element.74, f32[512,512]{1,0:T(8,128)} %get-tuple-element.75), kind=kOutput, calls=%fused_computation.11 | convolution fusion | flops 6442975232 | bytes 8388608 | tf_op jit(solution)/shard_map/dot_general | solution.py:44
  34.4 3.0 %fusion.129 = (f32[127,8,512]{2,0,1:T(8,128)}, f32[127,8,512]{2,0,1:T(8,128)}) fusion(f32[128,8,1024]{2,0,1:T(8,128)S(1)} %fusion.2), kind=kLoop, calls=%fused_computation.186 | loop fusion | bytes 8323072 | tf_op jit(solution)/shard_map/slice | solution.py:109
  38.2 0.7 reduce.4
  38.9 2.5 %fusion.4 = f32[8,1024]{1,0:T(8,128)S(1)} fusion(f32[8,512]{1,0:T(8,128)S(1)} %reshape.280, f32[512,512]{1,0:T(8,128)S(1)} %get-tuple-element.74, f32[512,512]{1,0:T(8,128)} %get-tuple-element.75), kind=kOutput, calls=%fused_computation.18 | convolution fusion | flops 50855936 | bytes 2146304 | tf_op jit(solution)/shard_map/dot_general | solution.py:44
  41.4 4.4 %multiply_reduce_fusion.1 = (f32[128]{0:T(128)S(1)}, f32[128]{0:T(128)S(1)}) fusion(f32[128,8,1024]{2,0,1:T(8,128)} %copy-done, f32[127,8,512]{2,0,1:T(8,128)} %get-tuple-element.60, f32[1,8,512]{2,0,1:T(1,128)S(1)} %get-tuple-element.62, f32[127,8,512]{2,0,1:T(8,128)S(1)} %copy-done.1, f32[1,8,512]{2,0,1:T(1,128)S(1)} %get-tuple-element.61, ...), kind=kLoop, calls=%fused_computation.16 | loop fusion | flops 8388352 | bytes 8391680 | tf_op jit(solution)/shard_map/reduce_sum | solution.py:58
  46.9 12.3 %while.1 = (s32[]{:T(128)}, bf16[128,4096]{0,1:T(8,128)(2,1)S(1)}, s32[8,2]{0,1:T(2,128)S(1)}, bf16[8,128,128]{2,1,0:T(8,128)(2,1)S(1)}, s32[]{:T(128)}) while((s32[]{:T(128)}, bf16[128,4096]{0,1:T(8,128)(2,1)S(1)}, s32[8,2]{0,1:T(2,128)S(1)}, bf16[8,128,128]{2,1,0:T(8,128)(2,1)S(1)}, s32[]{:T(128)}) %tuple.48), condition=%wide.while_cond, body=%wide.while_body.sunk | while | flops 2 | bytes 196713 | solution.py:128
  47.6 0.7 constant_dynamic-slice_fusion.6
  48.5 0.6 slice.181
  49.1 0.7 constant_dynamic-slice_fusion.6
  50.7 0.7 constant_dynamic-slice_fusion.6
  51.6 0.6 slice.181
  52.2 0.7 constant_dynamic-slice_fusion.6
  53.7 0.7 constant_dynamic-slice_fusion.6
  54.7 0.6 slice.181
  55.3 0.7 constant_dynamic-slice_fusion.6
  56.2 0.6 slice.181
  56.8 0.7 constant_dynamic-slice_fusion.6
  57.7 0.6 slice.181
  58.3 0.7 constant_dynamic-slice_fusion.6
  59.2 1.0 scatter_fusion
  60.2 1.0 copy.93
  61.2 3.9 %all-to-all-start = ((bf16[4,2,128,128]{3,1,2,0:T(2,128)(2,1)}), bf16[4,2,128,128]{3,1,2,0:T(2,128)(2,1)S(1)}, u32[]{:S(2)}, u32[]{:S(2)}) async-start(bf16[4,2,128,128]{3,1,2,0:T(2,128)(2,1)} %copy.93), calls=%async_computation | async-start | bytes 524288 | tf_op jit(solution)/shard_map/all_to_all | solution.py:140
  65.1 6.0 %all-to-all-done = bf16[4,2,128,128]{3,1,2,0:T(2,128)(2,1)S(1)} async-done(((bf16[4,2,128,128]{3,1,2,0:T(2,128)(2,1)}), bf16[4,2,128,128]{3,1,2,0:T(2,128)(2,1)S(1)}, u32[]{:S(2)}, u32[]{:S(2)}) %all-to-all-start) | async-done | bytes 262176 | tf_op jit(solution)/shard_map/all_to_all | solution.py:140
  71.2 2.4 %convolution_bitcast_fusion = f32[1,128,32,128]{3,2,1,0:T(8,128)} fusion(f32[32,8,1]{0,1,2:T(8,128)S(1)} %convolution_bitcast_fusion.1, bf16[8,128,128]{2,0,1:T(8,128)(2,1)S(1)} %bitcast.153), kind=kOutput, calls=%fused_computation.19 | convolution fusion | flops 50331648 | bytes 2360320 | tf_op jit(solution)/shard_map/nm,mxy->nxy/dot_general | solution.py:163
  73.6 3.0 %copy.120 = f32[1,128,32,128]{1,3,2,0:T(8,128)} copy(f32[1,128,32,128]{3,2,1,0:T(8,128)} %convolution_bitcast_fusion) | data formatting | bytes 4194304 | tf_op jit(solution)/shard_map/reshape | solution.py:169
  76.6 2.1 %fusion.1 = bf16[128,4096]{0,1:T(8,128)(2,1)S(1)} fusion(f32[1,128,32,128]{1,3,2,0:T(8,128)} %copy.120, f32[4096]{0:T(1024)S(1)} %broadcast_bitcast_fusion, f32[128,4096]{0,1:T(8,128)S(1)} %select_add_fusion, f32[128]{0:T(128)S(1)} %get-tuple-element.57), kind=kLoop, calls=%fused_computation.10 | loop fusion | flops 4194304 | bytes 5259776 | tf_op jit(solution)/shard_map/convert_element_type | solution.py:173
  78.7 1.6 %copy.127 = bf16[1,128,4,1024]{1,0,2,3:T(2,128)(2,1)S(1)} copy(bf16[1,128,4,1024]{1,3,2,0:T(8,128)(2,1)S(1)} %bitcast.151) | data formatting | bytes 2097152 | tf_op jit(solution)/shard_map/reshape | solution.py:178
  80.3 1.2 %gather_fusion = bf16[4,128,128]{1,0,2:T(4,128)(2,1)S(1)} fusion(bf16[4,1,128,1024]{2,1,0,3:T(2,128)(2,1)S(1)} %bitcast.150, s32[4]{0:T(128)S(1)} %fusion.77), kind=kCustom, calls=%fused_computation | custom fusion | bytes 262208 | tf_op jit(solution)/shard_map/vmap()/gather | solution.py:180
  82.2 1.4 %reduce.5 = bf16[512,128]{1,0:T(8,128)(2,1)S(1)} reduce(bf16[512,1,1,128]{3,2,1,0:T(2,128)(2,1)S(1)} %bitcast.154, bf16[]{:T(256)} %broadcast.413), dimensions={1,2}, to_apply=%bitcast.142.reduce_sub_computation | reduce | bytes 262146
  83.7 11.0 %all_to_all.20 = bf16[4,2,8192]{2,1,0:T(2,128)(2,1)S(1)} all-to-all(bf16[4,2,8192]{2,1,0:T(2,128)(2,1)S(1)} %reshape.338), channel_id=1, replica_groups=mesh['groups'=2,'sec'=4,'tile'=2,'row'=2] {'sec'}, dimensions={0} | all-to-all | bytes 262144 | tf_op jit(solution)/shard_map/all_to_all | solution.py:185
  96.0 0.6 fusion.46
  96.7 0.6 fusion.37
  97.3 0.6 fusion.6
  97.9 0.6 fusion.7
  98.8 0.8 fusion.19
  99.5 0.7 fusion.21
  100.3 0.7 convolution_add_fusion.1
  101.0 0.8 convolution_subtract_fusion.2
  101.8 0.6 fusion.42
  102.4 0.7 fusion.9
  103.1 0.8 copy.110
  (80 shorter events, 9.0 us)
Async XLA Ops:
  15.3 10.0 %copy-start.2 = (s32[1,4,8,3]{2,1,3,0:T(4,128)S(1)}, s32[1,4,8,3]{2,1,3,0:T(4,128)}, u32[]{:S(2)}) copy-start(s32[1,4,8,3]{2,1,3,0:T(4,128)} %param.7) | copy-start | bytes 1156
  15.3 10.1 %copy-start.3 = (f32[1,4,8]{2,1,0:T(4,128)S(1)}, f32[1,4,8]{2,1,0:T(4,128)}, u32[]{:S(2)}) copy-start(f32[1,4,8]{2,1,0:T(4,128)} %param.8) | copy-start | bytes 388
  17.5 20.2 %collective-permute-start = (f32[1,4096]{1,0:T(1,128)S(1)}, f32[1,4096]{1,0:T(1,128)S(1)}, u32[]{:S(2)}, u32[]{:S(2)}) collective-permute-start(f32[1,4096]{1,0:T(1,128)S(1)} %copy.91), channel_id=1, source_target_pairs={{0,1},{1,2},{2,3},{4,5},{5,6},{6,7},{8,9},{9,10},{10,11},{12,13},{... | collective-permute-start | bytes 49160 | tf_op jit(solution)/shard_map/ppermute | solution.py:19
  34.4 3.2 %copy-start = (f32[128,8,1024]{2,0,1:T(8,128)}, f32[128,8,1024]{2,0,1:T(8,128)S(1)}, u32[]{:S(2)}) copy-start(f32[128,8,1024]{2,0,1:T(8,128)S(1)} %fusion.2) | copy-start | bytes 12582916
  38.9 2.5 %copy-start.1 = (f32[127,8,512]{2,0,1:T(8,128)S(1)}, f32[127,8,512]{2,0,1:T(8,128)}, u32[]{:S(2)}) copy-start(f32[127,8,512]{2,0,1:T(8,128)} %get-tuple-element.59) | copy-start | bytes 6242308
  46.9 18.2 %copy-start.4 = (s32[1,4]{1,0:T(1,128)S(1)}, s32[1,4]{1,0:T(1,128)}, u32[]{:S(2)}) copy-start(s32[1,4]{1,0:T(1,128)} %param.9) | copy-start | bytes 52
  61.2 9.9 %all-to-all-start = ((bf16[4,2,128,128]{3,1,2,0:T(2,128)(2,1)}), bf16[4,2,128,128]{3,1,2,0:T(2,128)(2,1)S(1)}, u32[]{:S(2)}, u32[]{:S(2)}) async-start(bf16[4,2,128,128]{3,1,2,0:T(2,128)(2,1)} %copy.93), calls=%async_computation | async-start | bytes 524288 | tf_op jit(solution)/shard_map/all_to_all | solution.py:140
where the time goes:
time: 104 us
  local copies, waits for them, and re-layouts  33.1 us (32%)
  other arithmetic  25.4 us (24%)
  matrix products  20.9 us (20%)
  blocking collectives  11 us (11%)
  starting transfers between devices  6.26 us (6%)
  waiting for transfers between devices  6 us (6%)
    gather x40, local copies, waits for them, and re-layouts  12 us
    all_to_all x1, blocking collectives, per_device(): lax.all_to_all(outbound, 'sec', split_axis=3, concat_axis=0, tiled=True)  11 us
    dot_general x2, matrix products, row_spectra(): jnp.dot(rows.reshape(row_count * (row_width // SEG), SEG), dft_table, pre...  10.5 us
    add x1, other arithmetic, align_rows(): aligned + jnp.where(delays[:, None] == shift_by, padded[:, shift_by:shift...  9.08 us
    all_to_all x1, waiting for transfers between devices, per_device(): lax.all_to_all(outgoing.reshape(owners, CAP, BLOCK, BLOCK), ('tile', 'row...  5.99 us
    neg x1, other arithmetic, row_spectra(): dft_table = jnp.concatenate([cosine_table, -sine_table], 1)  5.29 us
    unnamed x17, local copies, waits for them, and re-layouts  4.7 us
    reduce_sum x1, other arithmetic, jitter_estimate(): numerator = jnp.mean(weights * cross_term, axis=(1, 2))  4.36 us
  transfers between devices with their start and end apart: 2, of which 1 were waited for; matrix products, arithmetic and copies ran while one was open for 17% of the time, Pallas kernels for 0%

commit v1 on v0

v1 whole, which is shorter than its diff:
```python
import functools
import math

import jax
import jax.numpy as jnp
import numpy as np
from jax import lax
from jax.experimental import pallas as pl
from jax.experimental.pallas import tpu as pltpu
from jax.sharding import PartitionSpec as P

SEG = 512
PATCH = 128
BLOCK = 128
JMAX = 8
CAP = 2
LANES = 128
MESH = pl.DeviceIdType.MESH


def dft_tables(side):
    index = np.arange(side)
    angles = (index[:, None] * index[None, :] % side) * (2.0 * math.pi / side)
    cosine, sine = np.cos(angles), np.sin(angles)
    table = np.concatenate(
        [
            np.concatenate([cosine, sine], 1),
            np.concatenate([cosine, -sine], 1),
            np.concatenate([-sine, -cosine], 1),
        ],
        0,
    )
    high = table.astype(jnp.bfloat16)
    low = (table - high.astype(np.float64)).astype(jnp.bfloat16)
    return np.stack([high, low])


def dot(a, b):
    return jnp.dot(a, b, preferred_element_type=jnp.float32)


def split(a):
    high = a.astype(jnp.bfloat16)
    return high, (a - high.astype(jnp.float32)).astype(jnp.bfloat16)


def dot3(a, b):
    return dot(a[0], b[0]) + (dot(a[0], b[1]) + dot(a[1], b[0]))


def kernel(
    sizes,
    pixels,
    delays,
    drifts,
    weights,
    columns,
    tables_hbm,
    jitter_out,
    surfaces_out,
    raw,
    tables,
    delay_rows,
    aligned,
    slopes,
    cross_sums,
    energies,
    jitter_rows,
    halo_out,
    halo_in,
    outbox,
    arrived,
    patch_out,
    patch_in,
    freq,
    load_sem,
    table_sem,
    halo_send,
    halo_recv,
    block_send,
    block_recv,
    patch_send,
    patch_recv,
):
    sections, tiles, rows_axis, row_count, row_width, moves, chunks = sizes
    owners = tiles * rows_axis
    blocks = row_width // LANES
    groups = row_count // 8
    chunk_rows = row_count // chunks
    per_seg = SEG // LANES
    me = lax.axis_index("tile") * rows_axis + lax.axis_index("row")
    section = lax.axis_index("sec")

    def band_device(band):
        return {"tile": band // rows_axis, "row": band % rows_axis}

    table_copy = pltpu.make_async_copy(tables_hbm, tables, table_sem)
    loads = [
        pltpu.make_async_copy(
            pixels.at[0, pl.ds(c * chunk_rows, chunk_rows)],
            raw.at[pl.ds(c * chunk_rows, chunk_rows)],
            load_sem.at[c],
        )
        for c in range(chunks)
    ]
    loads[chunks - 1].start()
    for c in range(chunks - 1):
        loads[c].start()
    table_copy.start()

    barrier = pltpu.get_barrier_semaphore()
    for step in range(1, owners):
        pl.semaphore_signal(
            barrier, inc=1, device_id=band_device((me + step) % owners), device_id_type=MESH
        )
    for step in range(1, sections):
        pl.semaphore_signal(
            barrier, inc=1, device_id={"sec": (section + step) % sections}, device_id_type=MESH
        )

    lane = lax.broadcasted_iota(jnp.int32, (8, LANES), 1)
    first_lane, last_lane = lane == 0, lane == LANES - 1
    delay_rows[...] = jnp.broadcast_to(
        delays[...].astype(jnp.float32), (LANES, row_count)
    ).T
    zero = jnp.zeros((8, LANES), jnp.float32)
    for block in range(blocks):
        aligned[block, 0:8, :] = zero

    def align(start):
        delay = delay_rows[pl.ds(start, 8), :].astype(jnp.int32)
        values = [raw[pl.ds(start, 8), v * LANES : (v + 1) * LANES] for v in range(blocks)]
        distance = JMAX // 2
        while distance:
            chosen = (delay & distance) != 0
            kept = lane < LANES - distance
            turned = [pltpu.roll(x, LANES - distance, 1) for x in values] + [zero]
            values = [
                jnp.where(chosen, jnp.where(kept, turned[v], turned[v + 1]), values[v])
                for v in range(blocks)
            ]
            distance //= 2
        return values

    def differences(values):
        before = [pltpu.roll(x, 1, 1) for x in values]
        after = [pltpu.roll(x, LANES - 1, 1) for x in values]
        line, ring = [], []
        for v in range(blocks):
            left = jnp.where(first_lane, before[v - 1] if v else zero, before[v])
            right = jnp.where(last_lane, after[v + 1] if v < blocks - 1 else zero, after[v])
            line.append(right - left)
            if v % per_seg == 0:
                left = jnp.where(first_lane, before[v + per_seg - 1], before[v])
            if v % per_seg == per_seg - 1:
                right = jnp.where(last_lane, after[v - per_seg + 1], after[v])
            ring.append(right - left)
        return line, ring

    def total(terms):
        terms = list(terms)
        while len(terms) > 1:
            terms = [
                terms[i] + terms[i + 1] if i + 1 < len(terms) else terms[i]
                for i in range(0, len(terms), 2)
            ]
        return terms[0]

    loads[chunks - 1].wait()
    last = align(row_count - 8)
    for v in range(blocks):
        halo_out[v, :, :] = last[v]
    pl.semaphore_wait(barrier, owners + sections - 2)
    halo = pltpu.make_async_remote_copy(
        src_ref=halo_out.at[:, pl.ds(7, 1)],
        dst_ref=halo_in,
        send_sem=halo_send,
        recv_sem=halo_recv,
        device_id=band_device((me + 1) % owners),
        device_id_type=MESH,
    )
    halo.start()

    def group_step(g, carry):
        start = pl.multiple_of(g * 8, 8)
        values = align(start)
        for v in range(blocks):
            aligned[v, pl.ds(start + 8, 8), :] = values[v]
        line, ring = differences(values)
        for v in range(blocks):
            slopes[v, pl.ds(start, 8), :] = 0.5 * line[v]
        energies[pl.ds(start + 8, 8), :] = total(x * x for x in values)
        cross_sums[pl.ds(start, 8), :] = total(
            aligned[v, pl.ds(start + 7, 8), :] * ring[v] for v in range(blocks)
        )
        return carry

    per_chunk = groups // chunks
    for c in range(chunks):
        if c < chunks - 1:
            loads[c].wait()
        lax.fori_loop(c * per_chunk, (c + 1) * per_chunk, group_step, 0)

    def find(band, owner, rank):
        source, target, weight = jnp.int32(0), jnp.int32(-1), jnp.float32(0.0)
        seen = jnp.int32(0)
        for k in range(moves):
            hit = drifts[0, band, k, 1] == owner
            here = hit & (seen == rank)
            source = jnp.where(here, drifts[0, band, k, 0], source)
            target = jnp.where(here, drifts[0, band, k, 2], target)
            weight = jnp.where(here, weights[0, band, k], weight)
            seen = seen + hit.astype(jnp.int32)
        return source, target, weight

    _, ring0 = differences([aligned[v, 8:16, :] for v in range(blocks)])
    halo.wait_recv()
    is_first = me == 0
    above = [
        jnp.where(is_first, 0.0, jnp.broadcast_to(halo_in[v], (8, LANES))) for v in range(blocks)
    ]
    row = lax.broadcasted_iota(jnp.int32, (8, LANES), 0)
    cross_sums[0:8, :] = jnp.where(
        row == 0, total(above[v] * ring0[v] for v in range(blocks)), cross_sums[0:8, :]
    )
    energies[0:8, :] = total(a * a for a in above)
    segs = row_width // SEG
    numerator = jnp.sum(cross_sums[...], axis=1, keepdims=True) * (-0.5 / segs)
    power = jnp.sum(
        energies[8 : 8 + row_count, :] + energies[7 : 7 + row_count, :], axis=1, keepdims=True
    ) * (0.5 / segs)
    jitter_rows[...] = jnp.broadcast_to(numerator / (power + 1e-05), (row_count, LANES))
    jitter_out[...] = jitter_rows[...].T[0:1, :]

    def corrected(block):
        return (
            aligned[block, 8 : 8 + row_count, :] - jitter_rows[...] * slopes[block]
        ).astype(jnp.bfloat16)

    block_copies = []
    for step in range(owners - 1, -1, -1):
        owner = (me + step) % owners
        for rank in range(CAP):
            source, _, _ = find(me, owner, rank)
            value = corrected(source)
            if step:
                outbox[step, rank] = value
            else:
                arrived[me, rank] = value
        if step:
            copy = pltpu.make_async_remote_copy(
                src_ref=outbox.at[step],
                dst_ref=arrived.at[me],
                send_sem=block_send.at[step],
                recv_sem=block_recv.at[step],
                device_id=band_device(owner),
                device_id_type=MESH,
            )
            copy.start()
            block_copies.append(copy)

    incoming = []
    for band in range(owners):
        for rank in range(CAP):
            _, target, weight = find(band, me, rank)
            incoming.append((band, rank, target, weight))
    for copy in block_copies:
        copy.wait_recv()

    def merged(block):
        value = corrected(block).astype(jnp.float32)
        norm = jnp.float32(1.0)
        for band, rank, target, weight in incoming:
            share = jnp.where(target == block, weight, 0.0)
            value = value + share * arrived[band, rank].astype(jnp.float32)
            norm = norm + share
        return (value / jnp.full((row_count, LANES), norm)).astype(jnp.bfloat16)

    slab_blocks = blocks // sections
    place = lax.broadcasted_iota(jnp.int32, (2 * LANES, LANES), 0) - lax.broadcasted_iota(
        jnp.int32, (2 * LANES, LANES), 1
    )
    patch_copies = []
    for step in list(range(1, sections)) + [0]:
        slab = (section + step) % sections
        offset = columns[0, slab]
        block = slab * slab_blocks + offset // LANES
        pair = jnp.concatenate([merged(block), merged(jnp.minimum(block + 1, blocks - 1))], 1)
        pick = (place == offset % LANES).astype(jnp.float32).astype(jnp.bfloat16)
        patch = dot(pair, pick).astype(jnp.bfloat16)
        if step:
            patch_out[step] = patch
            copy = pltpu.make_async_remote_copy(
                src_ref=patch_out.at[step],
                dst_ref=patch_in.at[section],
                send_sem=patch_send.at[step],
                recv_sem=patch_recv.at[step],
                device_id={"sec": slab},
                device_id_type=MESH,
            )
            copy.start()
            patch_copies.append(copy)
        else:
            patch_in[section] = patch

    table_copy.wait()
    wide = tables[0, 0:PATCH, :], tables[1, 0:PATCH, :]
    square = tables[0, PATCH : 3 * PATCH, :], tables[1, PATCH : 3 * PATCH, :]
    for step in range(sections):
        if step:
            patch_copies[step - 1].wait_recv()
        source = (section - step + sections) % sections
        patch = patch_in[source]
        first = dot(patch, wide[0]) + dot(patch, wide[1])
        stacked = jnp.concatenate([first[:, :PATCH], first[:, PATCH:]], 0)
        freq[source] = dot3(square, split(stacked))
    for s in range(sections - 1):
        now_real, now_imag = freq[s, 0:PATCH], freq[s, PATCH : 2 * PATCH]
        next_real, next_imag = freq[s + 1, 0:PATCH], freq[s + 1, PATCH : 2 * PATCH]
        cross_real = now_real * next_real + now_imag * next_imag
        cross_imag = now_imag * next_real - now_real * next_imag
        magnitude = jnp.sqrt(cross_real * cross_real + cross_imag * cross_imag)
        mean = jnp.sum(jnp.sum(magnitude, axis=0, keepdims=True), axis=1, keepdims=True) * (
            1.0 / (PATCH * PATCH)
        )
        scaled = 1.0 / (magnitude + (0.5 * mean + 1e-06))
        damped = jnp.concatenate([cross_real * scaled, cross_imag * scaled], 1)
        back = dot3(split(damped), square)
        stacked = jnp.concatenate([back[:, :PATCH], back[:, PATCH:]], 0)
        surfaces_out[s, 0, 0] = dot3(wide, split(stacked)) * (1.0 / PATCH)

    halo.wait_send()
    for copy in block_copies + patch_copies:
        copy.wait_send()


def per_device(section_pixels, jitter_index, drift_list, blend_weight, patch_col):
    _, row_count, row_width = section_pixels.shape
    sections = lax.axis_size("sec")
    tiles, rows_axis = lax.axis_size("tile"), lax.axis_size("row")
    owners = tiles * rows_axis
    moves = drift_list.shape[2]
    blocks = row_width // LANES
    chunks = 4
    sizes = (sections, tiles, rows_axis, row_count, row_width, moves, chunks)
    tables = jnp.asarray(dft_tables(PATCH))
    f32, bf16 = jnp.float32, jnp.bfloat16
    vmem = pl.BlockSpec(memory_space=pltpu.VMEM)
    smem = pl.BlockSpec(memory_space=pltpu.SMEM)
    anywhere = pl.BlockSpec(memory_space=pl.ANY)
    dma = pltpu.SemaphoreType.DMA
    return pl.pallas_call(
        functools.partial(kernel, sizes),
        out_shape=(
            jax.ShapeDtypeStruct((1, row_count), f32),
            jax.ShapeDtypeStruct((sections - 1, 1, 1, PATCH, PATCH), f32),
        ),
        in_specs=[anywhere, vmem, smem, smem, smem, anywhere],
        out_specs=(vmem, vmem),
        scratch_shapes=[
            pltpu.VMEM((row_count, row_width), f32),
            pltpu.VMEM(tables.shape, bf16),
            pltpu.VMEM((row_count, LANES), f32),
            pltpu.VMEM((blocks, row_count + 8, LANES), f32),
            pltpu.VMEM((blocks, row_count, LANES), f32),
            pltpu.VMEM((row_count, LANES), f32),
            pltpu.VMEM((row_count + 8, LANES), f32),
            pltpu.VMEM((row_count, LANES), f32),
            pltpu.VMEM((blocks, 8, LANES), f32),
            pltpu.VMEM((blocks, 1, LANES), f32),
            pltpu.VMEM((owners, CAP, BLOCK, BLOCK), bf16),
            pltpu.VMEM((owners, CAP, BLOCK, BLOCK), bf16),
            pltpu.VMEM((sections, PATCH, PATCH), bf16),
            pltpu.VMEM((sections, PATCH, PATCH), bf16),
            pltpu.VMEM((sections, 2 * PATCH, PATCH), f32),
            dma((chunks,)),
            dma,
            dma,
            dma,
            dma((owners,)),
            dma((owners,)),
            dma((sections,)),
            dma((sections,)),
        ],
        compiler_params=pltpu.CompilerParams(collective_id=0, has_side_effects=True),
        name="section_correlation",
    )(section_pixels, jitter_index, drift_list, blend_weight, patch_col, tables)


def solution(mesh):
    in_specs = (
        P(("groups", "sec"), ("tile", "row"), None),
        P(("groups", "sec"), ("tile", "row")),
        P(("groups", "sec"), None, None, None),
        P(("groups", "sec"), None, None),
        P(("tile", "row"), "groups"),
    )
    out_specs = (
        P(("groups", "sec"), ("tile", "row")),
        P("groups", ("tile", "row"), "sec", None, None),
    )
    return jax.shard_map(
        per_device, mesh=mesh, in_specs=in_specs, out_specs=out_specs, check_vma=False
    )
```

time: 104 us -> 28.8 us (0.28)
  local copies, waits for them, and re-layouts: 33.1 us -> 4.13 us
  other arithmetic: 25.4 us -> 0 us
  Pallas kernels: 0 us -> 23.8 us
  matrix products: 20.9 us -> 0 us
  blocking collectives: 11 us -> 0 us
  starting transfers between devices: 6.26 us -> 0 us
  waiting for transfers between devices: 6 us -> 0 us
    pallas_call x0 -> x1, Pallas kernels: none -> 23.8 us  [per_device(): pl.pallas_call(functools.partial(kernel, sizes), out_shape=(jax.ShapeDtyp...]
    dot_general x16 -> x0, matrix products: 20.9 us -> none  [the longest x2 10.5 us: row_spectra(): jnp.dot(rows.reshape(row_count * (row_width // SEG), SEG), dft_table, pre...]
    gather x41 -> x0, local copies, waits for them, and re-layouts: 13.2 us -> none
    all_to_all x1 -> x0, blocking collectives: 11 us -> none  [per_device(): lax.all_to_all(outbound, 'sec', split_axis=3, concat_axis=0, tiled=True)]
    add x4 -> x0, other arithmetic: 9.17 us -> none  [the longest x1 9.08 us: align_rows(): aligned + jnp.where(delays[:, None] == shift_by, padded[:, shift_by:shift...]
    slice x5 -> x0, local copies, waits for them, and re-layouts: 7.19 us -> none  [the longest x2 4.19 us: per_device(): above_row = shifted(aligned[row_count - 1:], ('tile', 'row'), 1)]
    all_to_all x1 -> x0, waiting for transfers between devices: 5.99 us -> none  [per_device(): lax.all_to_all(outgoing.reshape(owners, CAP, BLOCK, BLOCK), ('tile', 'row...]
    reshape x6 -> x0, local copies, waits for them, and re-layouts: 5.78 us -> none  [the longest x1 2.97 us: per_device(): incoming = incoming.reshape(band_rows, blocks_across, BLOCK, BLOCK).trans...]
  transfers between devices with their start and end apart: 2 -> 0, of which waited for: 1 -> 0; matrix products, arithmetic and copies ran while one was open for 17% -> 0% of each run, Pallas kernels for 0% -> 0%
where the time goes in v1:
time: 28.8 us; the launch traced here: 28.6 us
  Pallas kernels  23.8 us (83%)
  local copies, waits for them, and re-layouts  4.13 us (14%)
  between operations  0.64 us (2%)
    pallas_call x1, Pallas kernels, per_device(): pl.pallas_call(functools.partial(kernel, sizes), out_shape=(jax.ShapeDtyp...  23.8 us
    unnamed x3, local copies, waits for them, and re-layouts  4.13 us

profile of v1, /device:TPU:0, one launch (start us, length us, event | category | flops | bytes accessed | tf_op | source)
XLA Modules:
  0.0 28.6 jit_solution(10462454313905185105)
XLA Ops:
  0.6 1.4 %copy.8.drifts = s32[1,4,8,3]{3,2,1,0:T(8,128)} copy(s32[1,4,8,3]{2,1,3,0:T(4,128)} %param.8) | data formatting | bytes 768 | tf_op args[2]
  2.0 23.8 %section_correlation.1 = (f32[1,128]{1,0:T(1,128)}, f32[3,1,1,128,128]{4,3,2,1,0:T(8,128)}) custom-call(f32[1,128,4096]{2,1,0:T(8,128)} %pixels.1, s32[1,128]{1,0:T(1,128)} %delays.1, s32[1,4,8,3]{3,2,1,0:T(8,128)} %copy.8.drifts, f32[1,4,8]{2,1,0:T(4,128)} %weights.1, s32[1,4]{1,0:T(1,128)} %columns.1, bf16[2,384,256]{2,1,0:T(8,128)(2,1)} %constant.2.clone.tables_hbm), custom_call_target="tpu_custom_call" | custom-call | tf_op jit(solution)/shard_map/section_correlation/pallas_call | solution.py:352
  25.8 1.1 %copy.11 = f32[1,128]{1,0:T(1,128)} copy(f32[1,128]{1,0:T(1,128)} %get-tuple-element.4) | data formatting | bytes 1024
  26.9 1.6 %copy.12 = f32[3,1,1,128,128]{4,3,2,1,0:T(8,128)} copy(f32[3,1,1,128,128]{4,3,2,1,0:T(8,128)} %get-tuple-element.5) | data formatting | bytes 393216

commit v2 on v1

--- a/solution.py
+++ b/solution.py
@@ -12,7 +12,6 @@
 SEG = 512
 PATCH = 128
 BLOCK = 128
-JMAX = 8
 CAP = 2
 LANES = 128
 MESH = pl.DeviceIdType.MESH
@@ -51,15 +50,19 @@
 def kernel(
     sizes,
     pixels,
+    delays_hbm,
+    drifts_hbm,
+    weights_hbm,
+    columns_hbm,
+    tables_hbm,
+    jitter_out,
+    freq,
+    raw,
+    tables,
     delays,
     drifts,
     weights,
     columns,
-    tables_hbm,
-    jitter_out,
-    surfaces_out,
-    raw,
-    tables,
     delay_rows,
     aligned,
     slopes,
@@ -70,11 +73,12 @@
     halo_in,
     outbox,
     arrived,
+    blend,
     patch_out,
     patch_in,
-    freq,
     load_sem,
     table_sem,
+    small_sem,
     halo_send,
     halo_recv,
     block_send,
@@ -88,11 +92,25 @@
     groups = row_count // 8
     chunk_rows = row_count // chunks
     per_seg = SEG // LANES
-    me = lax.axis_index("tile") * rows_axis + lax.axis_index("row")
+    tile, row_at = lax.axis_index("tile"), lax.axis_index("row")
+    me = tile * rows_axis + row_at
     section = lax.axis_index("sec")
 
     def band_device(band):
         return {"tile": band // rows_axis, "row": band % rows_axis}
+
+    band_steps = [(t, r) for t in range(tiles) for r in range(rows_axis)][1:]
+    band_steps.sort(key=lambda step: -min(step[0], tiles - step[0]))
+
+    def band_at(step):
+        return (tile + step[0]) % tiles * rows_axis + (row_at + step[1]) % rows_axis
+
+    def band_from(step):
+        return (tile - step[0] + tiles) % tiles * rows_axis + (
+            row_at - step[1] + rows_axis
+        ) % rows_axis
+
+    section_steps = sorted(range(1, sections), key=lambda step: -min(step, sections - step))
 
     table_copy = pltpu.make_async_copy(tables_hbm, tables, table_sem)
     loads = [
@@ -103,9 +121,23 @@
         )
         for c in range(chunks)
     ]
+    small_copies = [
+        pltpu.make_async_copy(source, target, small_sem.at[i])
+        for i, (source, target) in enumerate(
+            (
+                (delays_hbm, delays),
+                (drifts_hbm, drifts),
+                (weights_hbm, weights),
+                (columns_hbm, columns),
+            )
+        )
+    ]
+    small_copies[0].start()
     loads[chunks - 1].start()
     for c in range(chunks - 1):
         loads[c].start()
+    for copy in small_copies[1:]:
+        copy.start()
     table_copy.start()
 
     barrier = pltpu.get_barrier_semaphore()
@@ -120,6 +152,7 @@
 
     lane = lax.broadcasted_iota(jnp.int32, (8, LANES), 1)
     first_lane, last_lane = lane == 0, lane == LANES - 1
+    small_copies[0].wait()
     delay_rows[...] = jnp.broadcast_to(
         delays[...].astype(jnp.float32), (LANES, row_count)
     ).T
@@ -130,16 +163,11 @@
     def align(start):
         delay = delay_rows[pl.ds(start, 8), :].astype(jnp.int32)
         values = [raw[pl.ds(start, 8), v * LANES : (v + 1) * LANES] for v in range(blocks)]
-        distance = JMAX // 2
-        while distance:
-            chosen = (delay & distance) != 0
-            kept = lane < LANES - distance
-            turned = [pltpu.roll(x, LANES - distance, 1) for x in values] + [zero]
-            values = [
-                jnp.where(chosen, jnp.where(kept, turned[v], turned[v + 1]), values[v])
-                for v in range(blocks)
-            ]
-            distance //= 2
+        index = lane + delay
+        kept = index < LANES
+        index = index & (LANES - 1)
+        turned = [jnp.take_along_axis(x, index, axis=1) for x in values] + [zero]
+        values = [jnp.where(kept, turned[v], turned[v + 1]) for v in range(blocks)]
         return values
 
     def differences(values):
@@ -205,13 +233,20 @@
         source, target, weight = jnp.int32(0), jnp.int32(-1), jnp.float32(0.0)
         seen = jnp.int32(0)
         for k in range(moves):
-            hit = drifts[0, band, k, 1] == owner
+            hit = drifts[0, 1, band, k] == owner
             here = hit & (seen == rank)
-            source = jnp.where(here, drifts[0, band, k, 0], source)
-            target = jnp.where(here, drifts[0, band, k, 2], target)
+            source = jnp.where(here, drifts[0, 0, band, k], source)
+            target = jnp.where(here, drifts[0, 2, band, k], target)
             weight = jnp.where(here, weights[0, band, k], weight)
             seen = seen + hit.astype(jnp.int32)
         return source, target, weight
+
+    for copy in small_copies[1:]:
+        copy.wait()
+    sources = {}
+    for step in band_steps + [(0, 0)]:
+        for rank in range(CAP):
+            sources[step, rank] = find(me, band_at(step), rank)[0]
 
     _, ring0 = differences([aligned[v, 8:16, :] for v in range(blocks)])
     halo.wait_recv()
@@ -237,84 +272,109 @@
             aligned[block, 8 : 8 + row_count, :] - jitter_rows[...] * slopes[block]
         ).astype(jnp.bfloat16)
 
-    block_copies = []
-    for step in range(owners - 1, -1, -1):
-        owner = (me + step) % owners
+    block_copies = {}
+    for step in band_steps:
+        slot = step[0] * rows_axis + step[1]
         for rank in range(CAP):
-            source, _, _ = find(me, owner, rank)
-            value = corrected(source)
-            if step:
-                outbox[step, rank] = value
-            else:
-                arrived[me, rank] = value
-        if step:
-            copy = pltpu.make_async_remote_copy(
-                src_ref=outbox.at[step],
-                dst_ref=arrived.at[me],
-                send_sem=block_send.at[step],
-                recv_sem=block_recv.at[step],
-                device_id=band_device(owner),
-                device_id_type=MESH,
-            )
-            copy.start()
-            block_copies.append(copy)
-
-    incoming = []
-    for band in range(owners):
+            outbox[slot, rank] = corrected(sources[step, rank])
+        copy = pltpu.make_async_remote_copy(
+            src_ref=outbox.at[slot],
+            dst_ref=arrived.at[slot],
+            send_sem=block_send.at[slot],
+            recv_sem=block_recv.at[slot],
+            device_id=band_device(band_at(step)),
+            device_id_type=MESH,
+        )
+        copy.start()
+        block_copies[step] = copy
+
+    slab_blocks = blocks // sections
+    slabs = [(section + step) % sections for step in range(sections)]
+    offsets = [columns[0, slab] for slab in slabs]
+    under = []
+    for step in range(sections):
+        block = slabs[step] * slab_blocks + offsets[step] // LANES
+        under += [block, jnp.minimum(block + 1, blocks - 1)]
+    norms = [jnp.float32(1.0)] * len(under)
+    shares = {}
+    for step in [(0, 0)] + band_steps:
         for rank in range(CAP):
-            _, target, weight = find(band, me, rank)
-            incoming.append((band, rank, target, weight))
-    for copy in block_copies:
-        copy.wait_recv()
-
-    def merged(block):
+            _, target, weight = find(band_from(step), me, rank)
+            shares[step, rank] = [jnp.where(target == block, weight, 0.0) for block in under]
+            norms = [norm + share for norm, share in zip(norms, shares[step, rank])]
+    own = [corrected(sources[(0, 0), rank]).astype(jnp.float32) for rank in range(CAP)]
+    for i, block in enumerate(under):
         value = corrected(block).astype(jnp.float32)
-        norm = jnp.float32(1.0)
-        for band, rank, target, weight in incoming:
-            share = jnp.where(target == block, weight, 0.0)
-            value = value + share * arrived[band, rank].astype(jnp.float32)
-            norm = norm + share
-        return (value / jnp.full((row_count, LANES), norm)).astype(jnp.bfloat16)
-
-    slab_blocks = blocks // sections
+        for rank in range(CAP):
+            value = value + shares[(0, 0), rank][i] * own[rank]
+        blend[i] = value
+
+    def with_shares(step, i, value, rows):
+        slot = step[0] * rows_axis + step[1]
+        for rank in range(CAP):
+            value = value + shares[step, rank][i] * arrived[slot, rank, rows, :].astype(jnp.float32)
+        return value
+
+    part = row_count // 4
+    for step in band_steps[:0:-1]:
+        block_copies[step].wait_recv()
+        for p in range(4):
+            rows = slice(p * part, (p + 1) * part)
+            for i in range(len(under)):
+                blend[i, rows, :] = with_shares(step, i, blend[i, rows, :], rows)
+    last_step = band_steps[0]
+    block_copies[last_step].wait_recv()
+
+    def merged(i):
+        value = with_shares(last_step, i, blend[i], slice(0, row_count))
+        share = 1.0 / jnp.full((8, LANES), norms[i])
+        return (value * share[0:1, :]).astype(jnp.bfloat16)
+
     place = lax.broadcasted_iota(jnp.int32, (2 * LANES, LANES), 0) - lax.broadcasted_iota(
         jnp.int32, (2 * LANES, LANES), 1
     )
-    patch_copies = []
-    for step in list(range(1, sections)) + [0]:
-        slab = (section + step) % sections
-        offset = columns[0, slab]
-        block = slab * slab_blocks + offset // LANES
-        pair = jnp.concatenate([merged(block), merged(jnp.minimum(block + 1, blocks - 1))], 1)
-        pick = (place == offset % LANES).astype(jnp.float32).astype(jnp.bfloat16)
+    patch_copies = {}
+    for step in section_steps + [0]:
+        pair = jnp.concatenate([merged(2 * step), merged(2 * step + 1)], 1)
+        pick = (place == offsets[step] % LANES).astype(jnp.float32).astype(jnp.bfloat16)
         patch = dot(pair, pick).astype(jnp.bfloat16)
         if step:
             patch_out[step] = patch
             copy = pltpu.make_async_remote_copy(
                 src_ref=patch_out.at[step],
-                dst_ref=patch_in.at[section],
+                dst_ref=patch_in.at[step],
                 send_sem=patch_send.at[step],
                 recv_sem=patch_recv.at[step],
-                device_id={"sec": slab},
+                device_id={"sec": slabs[step]},
                 device_id_type=MESH,
             )
             copy.start()
-            patch_copies.append(copy)
+            patch_copies[step] = copy
         else:
-            patch_in[section] = patch
+            patch_in[0] = patch
 
     table_copy.wait()
     wide = tables[0, 0:PATCH, :], tables[1, 0:PATCH, :]
     square = tables[0, PATCH : 3 * PATCH, :], tables[1, PATCH : 3 * PATCH, :]
-    for step in range(sections):
+    for step in [0] + section_steps[::-1]:
         if step:
-            patch_copies[step - 1].wait_recv()
+            patch_copies[step].wait_recv()
         source = (section - step + sections) % sections
-        patch = patch_in[source]
+        patch = patch_in[step]
         first = dot(patch, wide[0]) + dot(patch, wide[1])
         stacked = jnp.concatenate([first[:, :PATCH], first[:, PATCH:]], 0)
         freq[source] = dot3(square, split(stacked))
-    for s in range(sections - 1):
+
+    halo.wait_send()
+    for copy in list(block_copies.values()) + list(patch_copies.values()):
+        copy.wait_send()
+
+
+def correlate(freq, tables, jitter, jitter_out, surfaces_out):
+    jitter_out[...] = jitter[...]
+    wide = tables[0:PATCH, :]
+    square = tables[PATCH : 3 * PATCH, :]
+    for s in range(freq.shape[0] - 1):
         now_real, now_imag = freq[s, 0:PATCH], freq[s, PATCH : 2 * PATCH]
         next_real, next_imag = freq[s + 1, 0:PATCH], freq[s + 1, PATCH : 2 * PATCH]
         cross_real = now_real * next_real + now_imag * next_imag
@@ -325,13 +385,9 @@
         )
         scaled = 1.0 / (magnitude + (0.5 * mean + 1e-06))
         damped = jnp.concatenate([cross_real * scaled, cross_imag * scaled], 1)
-        back = dot3(split(damped), square)
+        back = dot(damped.astype(jnp.bfloat16), square)
         stacked = jnp.concatenate([back[:, :PATCH], back[:, PATCH:]], 0)
-        surfaces_out[s, 0, 0] = dot3(wide, split(stacked)) * (1.0 / PATCH)
-
-    halo.wait_send()
-    for copy in block_copies + patch_copies:
-        copy.wait_send()
+        surfaces_out[s, 0, 0] = dot(wide, stacked.astype(jnp.bfloat16)) * (1.0 / PATCH)
 
 
 def per_device(section_pixels, jitter_index, drift_list, blend_weight, patch_col):
@@ -343,23 +399,26 @@
     blocks = row_width // LANES
     chunks = 4
     sizes = (sections, tiles, rows_axis, row_count, row_width, moves, chunks)
-    tables = jnp.asarray(dft_tables(PATCH))
+    tables = dft_tables(PATCH)
     f32, bf16 = jnp.float32, jnp.bfloat16
     vmem = pl.BlockSpec(memory_space=pltpu.VMEM)
-    smem = pl.BlockSpec(memory_space=pltpu.SMEM)
     anywhere = pl.BlockSpec(memory_space=pl.ANY)
     dma = pltpu.SemaphoreType.DMA
-    return pl.pallas_call(
+    jitter, freq = pl.pallas_call(
         functools.partial(kernel, sizes),
         out_shape=(
             jax.ShapeDtypeStruct((1, row_count), f32),
-            jax.ShapeDtypeStruct((sections - 1, 1, 1, PATCH, PATCH), f32),
+            jax.ShapeDtypeStruct((sections, 2 * PATCH, PATCH), f32),
         ),
-        in_specs=[anywhere, vmem, smem, smem, smem, anywhere],
+        in_specs=[anywhere] * 6,
         out_specs=(vmem, vmem),
         scratch_shapes=[
             pltpu.VMEM((row_count, row_width), f32),
             pltpu.VMEM(tables.shape, bf16),
+            pltpu.VMEM(jitter_index.shape, jnp.int32),
+            pltpu.SMEM((1, 3, owners, moves), jnp.int32),
+            pltpu.SMEM(blend_weight.shape, f32),
+            pltpu.SMEM(patch_col.shape, jnp.int32),
             pltpu.VMEM((row_count, LANES), f32),
             pltpu.VMEM((blocks, row_count + 8, LANES), f32),
             pltpu.VMEM((blocks, row_count, LANES), f32),
@@ -370,11 +429,12 @@
             pltpu.VMEM((blocks, 1, LANES), f32),
             pltpu.VMEM((owners, CAP, BLOCK, BLOCK), bf16),
             pltpu.VMEM((owners, CAP, BLOCK, BLOCK), bf16),
+            pltpu.VMEM((2 * sections, BLOCK, BLOCK), f32),
             pltpu.VMEM((sections, PATCH, PATCH), bf16),
             pltpu.VMEM((sections, PATCH, PATCH), bf16),
-            pltpu.VMEM((sections, 2 * PATCH, PATCH), f32),
             dma((chunks,)),
             dma,
+            dma((4,)),
             dma,
             dma,
             dma((owners,)),
@@ -383,8 +443,25 @@
             dma((sections,)),
         ],
         compiler_params=pltpu.CompilerParams(collective_id=0, has_side_effects=True),
+        name="section_patches",
+    )(
+        section_pixels,
+        jitter_index,
+        jnp.transpose(drift_list, (0, 3, 1, 2)),
+        blend_weight,
+        patch_col,
+        tables,
+    )
+    return pl.pallas_call(
+        correlate,
+        out_shape=(
+            jax.ShapeDtypeStruct((1, row_count), f32),
+            jax.ShapeDtypeStruct((sections - 1, 1, 1, PATCH, PATCH), f32),
+        ),
+        in_specs=[vmem] * 3,
+        out_specs=(vmem, vmem),
         name="section_correlation",
-    )(section_pixels, jitter_index, drift_list, blend_weight, patch_col, tables)
+    )(freq, tables[0], jitter)
 
 
 def solution(mesh):

time: 28.8 us -> 22.9 us (0.80)
  local copies, waits for them, and re-layouts: 4.13 us -> 0 us
  Pallas kernels: 23.8 us -> 22.1 us
    pallas_call x1, Pallas kernels: 23.8 us -> 19.6 us  [per_device(): pl.pallas_call(functools.partial(kernel, sizes), out_shape=(jax.ShapeDtyp...]
    unnamed x3 -> x0, local copies, waits for them, and re-layouts: 4.13 us -> none
    pallas_call x0 -> x1, Pallas kernels: none -> 2.49 us  [per_device(): pl.pallas_call(correlate, out_shape=(jax.ShapeDtypeStruct((1, row_count),...]
where the time goes in v2:
time: 22.9 us; the launch traced here: 22.8 us
  Pallas kernels  22.1 us (97%)
  between operations  0.64 us (3%)
    pallas_call x1, Pallas kernels, per_device(): pl.pallas_call(functools.partial(kernel, sizes), out_shape=(jax.ShapeDtyp...  19.6 us
    pallas_call x1, Pallas kernels, per_device(): pl.pallas_call(correlate, out_shape=(jax.ShapeDtypeStruct((1, row_count),...  2.49 us

profile of v2, /device:TPU:0, one launch (start us, length us, event | category | flops | bytes accessed | tf_op | source)
XLA Modules:
  0.0 22.8 jit_solution(2140494208290185135)
XLA Ops:
  0.6 19.6 %section_patches.1 = (f32[1,128]{1,0:T(1,128)}, f32[4,256,128]{2,1,0:T(8,128)}) custom-call(f32[1,128,4096]{2,1,0:T(8,128)} %pixels.1, s32[1,128]{1,0:T(1,128)} %delays_hbm.1, s32[1,3,4,8]{3,2,1,0:T(4,128)} %bitcast.1, f32[1,4,8]{2,1,0:T(4,128)} %weights_hbm.1, s32[1,4]{1,0:T(1,128)} %columns_hbm.1, bf16[2,384,256]{2,1,0:T(8,128)(2,1)} %constant.4.clone.tables_hbm), custom_call_target="tpu_custom_call" | custom-call | tf_op jit(solution)/shard_map/section_patches/pallas_call | solution.py:407
  20.3 2.5 %section_correlation.1 = (f32[1,128]{1,0:T(1,128)}, f32[3,1,1,128,128]{4,3,2,1,0:T(8,128)}) custom-call(f32[4,256,128]{2,1,0:T(8,128)} %get-tuple-element.4.freq, bf16[384,256]{1,0:T(8,128)(2,1)} %constant.5.clone.tables, f32[1,128]{1,0:T(1,128)} %get-tuple-element.5.jitter), custom_call_target="tpu_custom_call" | custom-call | tf_op jit(solution)/shard_map/section_correlation/pallas_call | solution.py:455

commit v3 on v2

--- a/solution.py
+++ b/solution.py
@@ -73,7 +73,6 @@
     halo_in,
     outbox,
     arrived,
-    blend,
     patch_out,
     patch_in,
     load_sem,
@@ -223,12 +222,6 @@
         )
         return carry
 
-    per_chunk = groups // chunks
-    for c in range(chunks):
-        if c < chunks - 1:
-            loads[c].wait()
-        lax.fori_loop(c * per_chunk, (c + 1) * per_chunk, group_step, 0)
-
     def find(band, owner, rank):
         source, target, weight = jnp.int32(0), jnp.int32(-1), jnp.float32(0.0)
         seen = jnp.int32(0)
@@ -248,6 +241,46 @@
         for rank in range(CAP):
             sources[step, rank] = find(me, band_at(step), rank)[0]
 
+    segs = row_width // SEG
+
+    def corrected(block, rows):
+        shifted = slice(rows.start + 8, rows.stop + 8)
+        return (
+            aligned[block, shifted, :] - jitter_rows[rows, :] * slopes[block, rows, :]
+        ).astype(jnp.bfloat16)
+
+    block_copies = {}
+
+    def finish_chunk(c):
+        rows = slice(c * chunk_rows, (c + 1) * chunk_rows)
+        numerator = jnp.sum(cross_sums[rows, :], axis=1, keepdims=True) * (-0.5 / segs)
+        power = energies[rows.start + 8 : rows.stop + 8, :]
+        power = power + energies[rows.start + 7 : rows.stop + 7, :]
+        power = jnp.sum(power, axis=1, keepdims=True) * (0.5 / segs)
+        jitter_rows[rows, :] = jnp.broadcast_to(numerator / (power + 1e-05), (chunk_rows, LANES))
+        for step in band_steps:
+            slot = step[0] * rows_axis + step[1]
+            for rank in range(CAP):
+                outbox[slot, rank, rows, :] = corrected(sources[step, rank], rows)
+            copy = pltpu.make_async_remote_copy(
+                src_ref=outbox.at[slot, :, pl.ds(rows.start, chunk_rows)],
+                dst_ref=arrived.at[slot, :, pl.ds(rows.start, chunk_rows)],
+                send_sem=block_send.at[slot, c],
+                recv_sem=block_recv.at[slot, c],
+                device_id=band_device(band_at(step)),
+                device_id_type=MESH,
+            )
+            copy.start()
+            block_copies[step, c] = copy
+
+    per_chunk = groups // chunks
+    for c in range(chunks):
+        if c < chunks - 1:
+            loads[c].wait()
+        lax.fori_loop(c * per_chunk, (c + 1) * per_chunk, group_step, 0)
+        if c:
+            finish_chunk(c)
+
     _, ring0 = differences([aligned[v, 8:16, :] for v in range(blocks)])
     halo.wait_recv()
     is_first = me == 0
@@ -259,34 +292,8 @@
         row == 0, total(above[v] * ring0[v] for v in range(blocks)), cross_sums[0:8, :]
     )
     energies[0:8, :] = total(a * a for a in above)
-    segs = row_width // SEG
-    numerator = jnp.sum(cross_sums[...], axis=1, keepdims=True) * (-0.5 / segs)
-    power = jnp.sum(
-        energies[8 : 8 + row_count, :] + energies[7 : 7 + row_count, :], axis=1, keepdims=True
-    ) * (0.5 / segs)
-    jitter_rows[...] = jnp.broadcast_to(numerator / (power + 1e-05), (row_count, LANES))
-    jitter_out[...] = jitter_rows[...].T[0:1, :]
-
-    def corrected(block):
-        return (
-            aligned[block, 8 : 8 + row_count, :] - jitter_rows[...] * slopes[block]
-        ).astype(jnp.bfloat16)
-
-    block_copies = {}
-    for step in band_steps:
-        slot = step[0] * rows_axis + step[1]
-        for rank in range(CAP):
-            outbox[slot, rank] = corrected(sources[step, rank])
-        copy = pltpu.make_async_remote_copy(
-            src_ref=outbox.at[slot],
-            dst_ref=arrived.at[slot],
-            send_sem=block_send.at[slot],
-            recv_sem=block_recv.at[slot],
-            device_id=band_device(band_at(step)),
-            device_id_type=MESH,
-        )
-        copy.start()
-        block_copies[step] = copy
+    finish_chunk(0)
+    chunk_order = list(range(1, chunks)) + [0]
 
     slab_blocks = blocks // sections
     slabs = [(section + step) % sections for step in range(sections)]
@@ -302,63 +309,57 @@
             _, target, weight = find(band_from(step), me, rank)
             shares[step, rank] = [jnp.where(target == block, weight, 0.0) for block in under]
             norms = [norm + share for norm, share in zip(norms, shares[step, rank])]
-    own = [corrected(sources[(0, 0), rank]).astype(jnp.float32) for rank in range(CAP)]
-    for i, block in enumerate(under):
-        value = corrected(block).astype(jnp.float32)
+    lanes = lax.broadcasted_iota(jnp.int32, (chunk_rows, LANES), 1)
+    patch_copies = {}
+    scales = [1.0 / jnp.full((1, LANES), norm) for norm in norms]
+    for c in chunk_order:
+        rows = slice(c * chunk_rows, (c + 1) * chunk_rows)
+        terms = {}
         for rank in range(CAP):
-            value = value + shares[(0, 0), rank][i] * own[rank]
-        blend[i] = value
-
-    def with_shares(step, i, value, rows):
-        slot = step[0] * rows_axis + step[1]
-        for rank in range(CAP):
-            value = value + shares[step, rank][i] * arrived[slot, rank, rows, :].astype(jnp.float32)
-        return value
-
-    part = row_count // 4
-    for step in band_steps[:0:-1]:
-        block_copies[step].wait_recv()
-        for p in range(4):
-            rows = slice(p * part, (p + 1) * part)
-            for i in range(len(under)):
-                blend[i, rows, :] = with_shares(step, i, blend[i, rows, :], rows)
-    last_step = band_steps[0]
-    block_copies[last_step].wait_recv()
-
-    def merged(i):
-        value = with_shares(last_step, i, blend[i], slice(0, row_count))
-        share = 1.0 / jnp.full((8, LANES), norms[i])
-        return (value * share[0:1, :]).astype(jnp.bfloat16)
-
-    place = lax.broadcasted_iota(jnp.int32, (2 * LANES, LANES), 0) - lax.broadcasted_iota(
-        jnp.int32, (2 * LANES, LANES), 1
-    )
-    patch_copies = {}
-    for step in section_steps + [0]:
-        pair = jnp.concatenate([merged(2 * step), merged(2 * step + 1)], 1)
-        pick = (place == offsets[step] % LANES).astype(jnp.float32).astype(jnp.bfloat16)
-        patch = dot(pair, pick).astype(jnp.bfloat16)
-        if step:
-            patch_out[step] = patch
-            copy = pltpu.make_async_remote_copy(
-                src_ref=patch_out.at[step],
-                dst_ref=patch_in.at[step],
-                send_sem=patch_send.at[step],
-                recv_sem=patch_recv.at[step],
-                device_id={"sec": slabs[step]},
-                device_id_type=MESH,
-            )
-            copy.start()
-            patch_copies[step] = copy
-        else:
-            patch_in[0] = patch
+            terms[(0, 0), rank] = corrected(sources[(0, 0), rank], rows).astype(jnp.float32)
+        for step in band_steps[::-1]:
+            block_copies[step, c].wait_recv()
+            slot = step[0] * rows_axis + step[1]
+            for rank in range(CAP):
+                terms[step, rank] = arrived[slot, rank, rows, :].astype(jnp.float32)
+
+        def merged(i):
+            value = corrected(under[i], rows).astype(jnp.float32)
+            for key, term in terms.items():
+                value = value + shares[key][i] * term
+            return value * scales[i]
+
+        for step in section_steps + [0]:
+            index = lanes + offsets[step] % LANES
+            turn = index & (LANES - 1)
+            patch = jnp.where(
+                index < LANES,
+                jnp.take_along_axis(merged(2 * step), turn, axis=1),
+                jnp.take_along_axis(merged(2 * step + 1), turn, axis=1),
+            ).astype(jnp.bfloat16)
+            if step:
+                patch_out[step, rows, :] = patch
+                copy = pltpu.make_async_remote_copy(
+                    src_ref=patch_out.at[step, pl.ds(rows.start, chunk_rows)],
+                    dst_ref=patch_in.at[step, pl.ds(rows.start, chunk_rows)],
+                    send_sem=patch_send.at[step, c],
+                    recv_sem=patch_recv.at[step, c],
+                    device_id={"sec": slabs[step]},
+                    device_id_type=MESH,
+                )
+                copy.start()
+                patch_copies[step, c] = copy
+            else:
+                patch_in[0, rows, :] = patch
+    jitter_out[...] = jitter_rows[...].T[0:1, :]
 
     table_copy.wait()
     wide = tables[0, 0:PATCH, :], tables[1, 0:PATCH, :]
     square = tables[0, PATCH : 3 * PATCH, :], tables[1, PATCH : 3 * PATCH, :]
     for step in [0] + section_steps[::-1]:
         if step:
-            patch_copies[step].wait_recv()
+            for c in chunk_order:
+                patch_copies[step, c].wait_recv()
         source = (section - step + sections) % sections
         patch = patch_in[step]
         first = dot(patch, wide[0]) + dot(patch, wide[1])
@@ -429,7 +430,6 @@
             pltpu.VMEM((blocks, 1, LANES), f32),
             pltpu.VMEM((owners, CAP, BLOCK, BLOCK), bf16),
             pltpu.VMEM((owners, CAP, BLOCK, BLOCK), bf16),
-            pltpu.VMEM((2 * sections, BLOCK, BLOCK), f32),
             pltpu.VMEM((sections, PATCH, PATCH), bf16),
             pltpu.VMEM((sections, PATCH, PATCH), bf16),
             dma((chunks,)),
@@ -437,10 +437,10 @@
             dma((4,)),
             dma,
             dma,
-            dma((owners,)),
-            dma((owners,)),
-            dma((sections,)),
-            dma((sections,)),
+            dma((owners, chunks)),
+            dma((owners, chunks)),
+            dma((sections, chunks)),
+            dma((sections, chunks)),
         ],
         compiler_params=pltpu.CompilerParams(collective_id=0, has_side_effects=True),
         name="section_patches",

time: 22.9 us -> 21.5 us (0.939)
  Pallas kernels: 22.1 us -> 20.7 us
    pallas_call x1, Pallas kernels: 19.6 us -> 18.2 us  [per_device(): pl.pallas_call(functools.partial(kernel, sizes), out_shape=(jax.ShapeDtyp...]
where the time goes in v3:
time: 21.5 us; the launch traced here: 21.3 us
  Pallas kernels  20.7 us (96%)
  between operations  0.64 us (3%)
    pallas_call x1, Pallas kernels, per_device(): pl.pallas_call(functools.partial(kernel, sizes), out_shape=(jax.ShapeDtyp...  18.2 us
    pallas_call x1, Pallas kernels, per_device(): pl.pallas_call(correlate, out_shape=(jax.ShapeDtypeStruct((1, row_count),...  2.49 us

profile of v3, /device:TPU:0, one launch (start us, length us, event | category | flops | bytes accessed | tf_op | source)
XLA Modules:
  0.0 21.3 jit_solution(4851147356542478758)
XLA Ops:
  0.6 18.2 %section_patches.1 = (f32[1,128]{1,0:T(1,128)}, f32[4,256,128]{2,1,0:T(8,128)}) custom-call(f32[1,128,4096]{2,1,0:T(8,128)} %pixels.1, s32[1,128]{1,0:T(1,128)} %delays_hbm.1, s32[1,3,4,8]{3,2,1,0:T(4,128)} %bitcast.1, f32[1,4,8]{2,1,0:T(4,128)} %weights_hbm.1, s32[1,4]{1,0:T(1,128)} %columns_hbm.1, bf16[2,384,256]{2,1,0:T(8,128)(2,1)} %constant.4.clone.tables_hbm), custom_call_target="tpu_custom_call" | custom-call | tf_op jit(solution)/shard_map/section_patches/pallas_call | solution.py:408
  18.8 2.5 %section_correlation.1 = (f32[1,128]{1,0:T(1,128)}, f32[3,1,1,128,128]{4,3,2,1,0:T(8,128)}) custom-call(f32[4,256,128]{2,1,0:T(8,128)} %get-tuple-element.4.freq, bf16[384,256]{1,0:T(8,128)(2,1)} %constant.5.clone.tables, f32[1,128]{1,0:T(1,128)} %get-tuple-element.5.jitter), custom_call_target="tpu_custom_call" | custom-call | tf_op jit(solution)/shard_map/section_correlation/pallas_call | solution.py:455

commit v4 on v3

--- a/solution.py
+++ b/solution.py
@@ -57,8 +57,8 @@
     tables_hbm,
     jitter_out,
     freq,
+    tables,
     raw,
-    tables,
     delays,
     drifts,
     weights,
@@ -273,6 +273,19 @@
             copy.start()
             block_copies[step, c] = copy
 
+    def finish_first():
+        _, ring0 = differences([aligned[v, 8:16, :] for v in range(blocks)])
+        halo.wait_recv()
+        is_first = me == 0
+        above = [
+            jnp.where(is_first, 0.0, jnp.broadcast_to(halo_in[v], (8, LANES))) for v in range(blocks)
+        ]
+        row = lax.broadcasted_iota(jnp.int32, (8, LANES), 0)
+        cross_sums[0:8, :] = jnp.where(
+            row == 0, total(above[v] * ring0[v] for v in range(blocks)), cross_sums[0:8, :]
+        )
+        energies[0:8, :] = total(a * a for a in above)
+        finish_chunk(0)
     per_chunk = groups // chunks
     for c in range(chunks):
         if c < chunks - 1:
@@ -280,20 +293,10 @@
         lax.fori_loop(c * per_chunk, (c + 1) * per_chunk, group_step, 0)
         if c:
             finish_chunk(c)
-
-    _, ring0 = differences([aligned[v, 8:16, :] for v in range(blocks)])
-    halo.wait_recv()
-    is_first = me == 0
-    above = [
-        jnp.where(is_first, 0.0, jnp.broadcast_to(halo_in[v], (8, LANES))) for v in range(blocks)
-    ]
-    row = lax.broadcasted_iota(jnp.int32, (8, LANES), 0)
-    cross_sums[0:8, :] = jnp.where(
-        row == 0, total(above[v] * ring0[v] for v in range(blocks)), cross_sums[0:8, :]
-    )
-    energies[0:8, :] = total(a * a for a in above)
-    finish_chunk(0)
-    chunk_order = list(range(1, chunks)) + [0]
+        if c == chunks - 2:
+            finish_first()
+
+    chunk_order = list(range(1, chunks - 1)) + [0, chunks - 1]
 
     slab_blocks = blocks // sections
     slabs = [(section + step) % sections for step in range(sections)]
@@ -356,15 +359,18 @@
     table_copy.wait()
     wide = tables[0, 0:PATCH, :], tables[1, 0:PATCH, :]
     square = tables[0, PATCH : 3 * PATCH, :], tables[1, PATCH : 3 * PATCH, :]
-    for step in [0] + section_steps[::-1]:
-        if step:
-            for c in chunk_order:
-                patch_copies[step, c].wait_recv()
-        source = (section - step + sections) % sections
+    def transform(step):
         patch = patch_in[step]
         first = dot(patch, wide[0]) + dot(patch, wide[1])
         stacked = jnp.concatenate([first[:, :PATCH], first[:, PATCH:]], 0)
-        freq[source] = dot3(square, split(stacked))
+        freq[(section - step + sections) % sections] = dot3(square, split(stacked))
+
+    transform(0)
+    for step in section_steps[::-1]:
+        for c in chunk_order:
+            patch_copies[step, c].wait_recv()
+    for step in section_steps[::-1]:
+        transform(step)
 
     halo.wait_send()
     for copy in list(block_copies.values()) + list(patch_copies.values()):
@@ -373,8 +379,8 @@
 
 def correlate(freq, tables, jitter, jitter_out, surfaces_out):
     jitter_out[...] = jitter[...]
-    wide = tables[0:PATCH, :]
-    square = tables[PATCH : 3 * PATCH, :]
+    wide = tables[0, 0:PATCH, :]
+    square = tables[0, PATCH : 3 * PATCH, :]
     for s in range(freq.shape[0] - 1):
         now_real, now_imag = freq[s, 0:PATCH], freq[s, PATCH : 2 * PATCH]
         next_real, next_imag = freq[s + 1, 0:PATCH], freq[s + 1, PATCH : 2 * PATCH]
@@ -405,17 +411,17 @@
     vmem = pl.BlockSpec(memory_space=pltpu.VMEM)
     anywhere = pl.BlockSpec(memory_space=pl.ANY)
     dma = pltpu.SemaphoreType.DMA
-    jitter, freq = pl.pallas_call(
+    between = pl.pallas_call(
         functools.partial(kernel, sizes),
         out_shape=(
-            jax.ShapeDtypeStruct((1, row_count), f32),
-            jax.ShapeDtypeStruct((sections, 2 * PATCH, PATCH), f32),
+            pltpu.VMEM((1, row_count), f32),
+            pltpu.VMEM((sections, 2 * PATCH, PATCH), f32),
+            pltpu.VMEM(tables.shape, bf16),
         ),
         in_specs=[anywhere] * 6,
-        out_specs=(vmem, vmem),
+        out_specs=(vmem, vmem, vmem),
         scratch_shapes=[
             pltpu.VMEM((row_count, row_width), f32),
-            pltpu.VMEM(tables.shape, bf16),
             pltpu.VMEM(jitter_index.shape, jnp.int32),
             pltpu.SMEM((1, 3, owners, moves), jnp.int32),
             pltpu.SMEM(blend_weight.shape, f32),
@@ -452,6 +458,7 @@
         patch_col,
         tables,
     )
+    jitter, freq, tables = [pltpu.with_memory_space_constraint(x, pltpu.VMEM) for x in between]
     return pl.pallas_call(
         correlate,
         out_shape=(
@@ -461,7 +468,7 @@
         in_specs=[vmem] * 3,
         out_specs=(vmem, vmem),
         name="section_correlation",
-    )(freq, tables[0], jitter)
+    )(freq, tables, jitter)
 
 
 def solution(mesh):

time: 21.5 us -> 19.4 us (0.902)
  Pallas kernels: 20.7 us -> 18.6 us
    pallas_call x1, Pallas kernels: 2.49 us -> 1.34 us  [per_device(): pl.pallas_call(correlate, out_shape=(jax.ShapeDtypeStruct((1, row_count),...]
    pallas_call x1, Pallas kernels: 18.2 us -> 17.3 us  [per_device(): pl.pallas_call(functools.partial(kernel, sizes), out_shape=(pltpu.VMEM((1...]
where the time goes in v4:
time: 19.4 us; the launch traced here: 19.3 us
  Pallas kernels  18.6 us (96%)
  between operations  0.64 us (3%)
    pallas_call x1, Pallas kernels, per_device(): pl.pallas_call(functools.partial(kernel, sizes), out_shape=(pltpu.VMEM((1...  17.3 us
    pallas_call x1, Pallas kernels, per_device(): pl.pallas_call(correlate, out_shape=(jax.ShapeDtypeStruct((1, row_count),...  1.34 us

profile of v4, /device:TPU:0, one launch (start us, length us, event | category | flops | bytes accessed | tf_op | source)
XLA Modules:
  0.0 19.3 jit_solution(10238223864698791952)
XLA Ops:
  0.6 17.3 %section_patches.1 = (f32[1,128]{1,0:T(1,128)S(1)}, f32[4,256,128]{2,1,0:T(8,128)S(1)}, bf16[2,384,256]{2,1,0:T(8,128)(2,1)S(1)}) custom-call(f32[1,128,4096]{2,1,0:T(8,128)} %pixels.1, s32[1,128]{1,0:T(1,128)} %delays_hbm.1, s32[1,3,4,8]{3,2,1,0:T(4,128)} %bitcast.1, f32[1,4,8]{2,1,0:T(4,128)} %weights_hbm.1, s32[1,4]{1,0:T(1,128)} %columns_hbm.1, ...), custom_call_target="tpu_custom_call" | custom-call | tf_op jit(solution)/shard_map/section_patches/pallas_call | solution.py:414
  17.9 1.3 %section_correlation.1 = (f32[1,128]{1,0:T(1,128)}, f32[3,1,1,128,128]{4,3,2,1,0:T(8,128)}) custom-call(f32[4,256,128]{2,1,0:T(8,128)S(1)} %get-tuple-element.5.freq, bf16[2,384,256]{2,1,0:T(8,128)(2,1)S(1)} %get-tuple-element.6.tables, f32[1,128]{1,0:T(1,128)S(1)} %get-tuple-element.7.jitter), custom_call_target="tpu_custom_call" | custom-call | tf_op jit(solution)/shard_map/section_correlation/pallas_call | solution.py:462

commit v5 on v4

--- a/solution.py
+++ b/solution.py
@@ -359,18 +359,23 @@
     table_copy.wait()
     wide = tables[0, 0:PATCH, :], tables[1, 0:PATCH, :]
     square = tables[0, PATCH : 3 * PATCH, :], tables[1, PATCH : 3 * PATCH, :]
-    def transform(step):
-        patch = patch_in[step]
-        first = dot(patch, wide[0]) + dot(patch, wide[1])
-        stacked = jnp.concatenate([first[:, :PATCH], first[:, PATCH:]], 0)
-        freq[(section - step + sections) % sections] = dot3(square, split(stacked))
-
-    transform(0)
+    def transform(steps):
+        patches = jnp.concatenate([patch_in[step] for step in steps], 0)
+        first = dot(patches, wide[0]) + dot(patches, wide[1])
+        stacked = [
+            jnp.concatenate([first[at : at + PATCH, :PATCH], first[at : at + PATCH, PATCH:]], 0)
+            for at in range(0, len(steps) * PATCH, PATCH)
+        ]
+        both = dot3(square, split(jnp.concatenate(stacked, 1)))
+        for i, step in enumerate(steps):
+            source = (section - step + sections) % sections
+            freq[source] = both[:, i * PATCH : (i + 1) * PATCH]
+
+    transform([0])
     for step in section_steps[::-1]:
         for c in chunk_order:
             patch_copies[step, c].wait_recv()
-    for step in section_steps[::-1]:
-        transform(step)
+    transform(section_steps[::-1])
 
     halo.wait_send()
     for copy in list(block_copies.values()) + list(patch_copies.values()):

time: 19.4 us -> 19.1 us (0.985)
  Pallas kernels: 18.6 us -> 18.3 us
    pallas_call x1, Pallas kernels: 17.3 us -> 17 us  [per_device(): pl.pallas_call(functools.partial(kernel, sizes), out_shape=(pltpu.VMEM((1...]
where the time goes in v5:
time: 19.1 us; the launch traced here: 19 us
  Pallas kernels  18.3 us (96%)
  between operations  0.64 us (3%)
    pallas_call x1, Pallas kernels, per_device(): pl.pallas_call(functools.partial(kernel, sizes), out_shape=(pltpu.VMEM((1...  17 us
    pallas_call x1, Pallas kernels, per_device(): pl.pallas_call(correlate, out_shape=(jax.ShapeDtypeStruct((1, row_count),...  1.34 us

profile of v5, /device:TPU:0, one launch (start us, length us, event | category | flops | bytes accessed | tf_op | source)
XLA Modules:
  0.0 19.0 jit_solution(4307998951002889450)
XLA Ops:
  0.6 17.0 %section_patches.1 = (f32[1,128]{1,0:T(1,128)S(1)}, f32[4,256,128]{2,1,0:T(8,128)S(1)}, bf16[2,384,256]{2,1,0:T(8,128)(2,1)S(1)}) custom-call(f32[1,128,4096]{2,1,0:T(8,128)} %pixels.1, s32[1,128]{1,0:T(1,128)} %delays_hbm.1, s32[1,3,4,8]{3,2,1,0:T(4,128)} %bitcast.1, f32[1,4,8]{2,1,0:T(4,128)} %weights_hbm.1, s32[1,4]{1,0:T(1,128)} %columns_hbm.1, ...), custom_call_target="tpu_custom_call" | custom-call | tf_op jit(solution)/shard_map/section_patches/pallas_call | solution.py:419
  17.6 1.3 %section_correlation.1 = (f32[1,128]{1,0:T(1,128)}, f32[3,1,1,128,128]{4,3,2,1,0:T(8,128)}) custom-call(f32[4,256,128]{2,1,0:T(8,128)S(1)} %get-tuple-element.5.freq, bf16[2,384,256]{2,1,0:T(8,128)(2,1)S(1)} %get-tuple-element.6.tables, f32[1,128]{1,0:T(1,128)S(1)} %get-tuple-element.7.jitter), custom_call_target="tpu_custom_call" | custom-call | tf_op jit(solution)/shard_map/section_correlation/pallas_call | solution.py:467
